TPU v7x, 32 devices: a whole 2x2x4 slice. The times are simulated.
32 devices in a mesh: win: 8 (over y, x, core), seq: 4 (over z).
Axes of the slice: x: 2, y: 2, z: 4, core: 2. Of those that a mesh axis runs over, the one named last changes fastest.
Arguments:
- qkv_grid: bfloat16 [90, 8, 32, 4608], P(None, 'win', 'seq'), may hold values from -160 to 160
- tokens: bfloat16 [90, 8, 32, 1536], P(None, 'win', 'seq'), may hold values from -6 to 6
- out_weight: bfloat16 [1536, 1536], replicated, may hold values from -0.625 to 0.625
- regions: int32 [90, 8, 32], P(None, 'win'), may hold values from 0 to 2, as said below
Outputs:
- mixed: bfloat16 [90, 8, 32, 1536], P(None, 'win', 'seq')
Inputs may be any that keep to these rules, and one draw needn't show every extreme that they name: `regions`: columns 2m and 2m+1 of a window always have the same region id.
All inputs are finite; a program needn't handle non-finite values.
Results may differ from a plain program's by a relative error of at most 0.01.
Values may be sent and summed in bfloat16 or wider, within the bound.
A program may use at most 128 MiB of HBM per device.

v0:
```python
import jax
import jax.numpy as jnp
from jax import lax
from jax.sharding import PartitionSpec as P

D = 1536
HEADS = 16
HD = 96
WH = 30
WW = 32


def from_behind(block, axis, distance):
    devices = range(lax.axis_size(axis))
    route = [((i - distance) % len(devices), i) for i in devices]
    return lax.ppermute(block, axis, route)


def attend(window_block, labels):
    queries = window_block[:, 0]
    key_rows = window_block[:, 1]
    values = window_block[:, 2]
    scores = jnp.einsum(
        "qhd,khd->hqk", queries, key_rows, preferred_element_type=jnp.float32
    ) * HD ** (-0.5)
    allowed = labels[:, None] == labels[None, :]
    scores = jnp.where(allowed[None], scores, -1e30)
    largest = jnp.max(scores, axis=-1, keepdims=True)
    weights = jnp.exp(scores - largest)
    soft_weights = (weights / jnp.sum(weights, axis=-1, keepdims=True)).astype(jnp.bfloat16)
    result = jnp.einsum("hqk,khd->qhd", soft_weights, values, preferred_element_type=jnp.float32)
    return result.astype(jnp.bfloat16)


def one_window(paired):
    return attend(paired[0], paired[1])


def window_attention(flat_grid, labels_flat):
    row_total, col_total, three, heads_here, head_size = flat_grid.shape
    bands = row_total // WH
    window_count = col_total // WW
    blocks = flat_grid.reshape(bands, WH, window_count, WW, three, heads_here, head_size)
    blocks = blocks.transpose(0, 2, 1, 3, 4, 5, 6).reshape(
        bands * window_count, WH * WW, three, heads_here, head_size
    )
    labels = (
        labels_flat.reshape(bands, WH, window_count, WW)
        .transpose(0, 2, 1, 3)
        .reshape(bands * window_count, WH * WW)
    )
    attended = lax.map(one_window, (blocks, labels))
    attended = attended.reshape(bands, window_count, WH, WW, heads_here, head_size).transpose(
        0, 2, 1, 3, 4, 5
    )
    return attended.reshape(row_total, col_total, heads_here, head_size)


def per_device(qkv_grid, tokens, out_weight, regions):
    seq_count = lax.axis_size("seq")
    lat_rows, win_count, col_count, packed_width = qkv_grid.shape
    labels_local = regions.reshape(lat_rows, win_count * WW)
    half_cols = WW // 2
    half_rows = WH // 2
    group_heads = HEADS // seq_count
    split_heads = qkv_grid.reshape(lat_rows, win_count, col_count, 3, seq_count, group_heads, HD)
    gathered = lax.all_to_all(split_heads, "seq", split_axis=4, concat_axis=2, tiled=True)
    flat_grid = gathered.reshape(lat_rows, win_count * WW, 3, group_heads, HD)
    arriving = from_behind(flat_grid[:, :half_cols], "win", -1)
    shifted = jnp.concatenate([flat_grid[:, half_cols:], arriving], axis=1)
    shifted = jnp.roll(shifted, -half_rows, axis=0)
    result = window_attention(shifted, labels_local)
    result = jnp.roll(result, half_rows, axis=0)
    leaving = from_behind(result[:, -half_cols:], "win", 1)
    result = jnp.concatenate([leaving, result[:, :-half_cols]], axis=1)
    attended = result.reshape(lat_rows, win_count, WW, 1, group_heads, HD)
    returned = lax.all_to_all(attended, "seq", split_axis=2, concat_axis=3, tiled=True)
    mixed_in = returned.reshape(lat_rows, win_count, col_count, D)
    projected = jnp.dot(mixed_in.reshape(-1, D), out_weight, preferred_element_type=jnp.float32)
    total = projected + tokens.reshape(-1, D).astype(jnp.float32)
    return total.astype(jnp.bfloat16).reshape(tokens.shape)


def solution(mesh):
    in_specs = (P(None, "win", "seq", None), P(None, "win", "seq", None), P(), P(None, "win", None))
    out_specs = P(None, "win", "seq", None)
    return jax.shard_map(
        per_device, mesh=mesh, in_specs=in_specs, out_specs=out_specs, check_vma=False
    )
```

profile of v0, /device:TPU:0, one launch (start us, length us, event | category | flops | bytes accessed | tf_op | source)
XLA Modules:
  0.0 490.2 jit_solution(6502701629563649295)
XLA Ops:
  0.0 17.0 %reshape.50 = bf16[90,1,8,3,4,4,96]{6,5,4,3,2,0,1:T(4,128)(2,1)} reshape(bf16[90,1,8,4608]{3,2,1,0:T(8,128)(2,1)} %param.6) | data formatting | bytes 13271040 | tf_op jit(solution)/shard_map/reshape | solution.py:66
  17.0 5.5 %copy.34 = bf16[90,1,8,3,4,4,96]{6,5,3,2,0,1,4:T(4,128)(2,1)S(1)} copy(bf16[90,1,8,3,4,4,96]{6,5,4,3,2,0,1:T(4,128)(2,1)} %reshape.50) | data formatting | bytes 13271040 | tf_op jit(solution)/shard_map/reshape | solution.py:66
  22.6 199.1 %all_to_all.30 = bf16[90,1,8,3,4,4,96]{6,5,3,2,0,1,4:T(4,128)(2,1)} all-to-all(bf16[90,1,8,3,4,4,96]{6,5,3,2,0,1,4:T(4,128)(2,1)S(1)} %copy.34), channel_id=1, replica_groups=mesh['win'=8,'seq'=4] {'seq'}, dimensions={4} | all-to-all | bytes 13271040 | tf_op jit(solution)/shard_map/all_to_all | solution.py:67
  221.7 9.7 %copy.46 = bf16[90,1,8,3,4,4,96]{6,2,4,5,3,0,1:T(8,128)(2,1)} copy(bf16[90,1,8,3,4,4,96]{6,5,3,2,0,1,4:T(4,128)(2,1)} %all_to_all.30) | data formatting | bytes 13271040 | tf_op jit(solution)/shard_map/all_to_all | solution.py:67
  231.4 9.3 %fusion.22 = (bf16[90,16,3,4,96]{4,1,3,2,0:T(8,128)(2,1)}, bf16[90,16,3,4,96]{4,1,3,2,0:T(8,128)(2,1)}) fusion(bf16[90,32,3,4,96]{4,1,3,2,0:T(8,128)(2,1)} %bitcast.76), kind=kLoop, calls=%fused_computation.39 | loop fusion | bytes 13271040 | tf_op jit(solution)/shard_map/slice | solution.py:70
  242.0 48.6 %collective-permute-done = bf16[90,16,3,4,96]{4,1,3,2,0:T(8,128)(2,1)} collective-permute-done((bf16[90,16,3,4,96]{4,1,3,2,0:T(8,128)(2,1)}, bf16[90,16,3,4,96]{4,1,3,2,0:T(8,128)(2,1)}, u32[]{:S(2)}, u32[]{:S(2)}) %collective-permute-start) | collective-permute-done | bytes 3317792 | tf_op jit(solution)/shard_map/ppermute | solution.py:16
  290.6 5.2 %fusion.15 = bf16[75,32,3,4,96]{4,1,3,2,0:T(8,128)(2,1)S(1)} fusion(bf16[90,16,3,4,96]{4,1,3,2,0:T(8,128)(2,1)} %get-tuple-element.54, bf16[90,16,3,4,96]{4,1,3,2,0:T(8,128)(2,1)} %collective-permute-done), kind=kLoop, calls=%fused_computation.27 | loop fusion | flops 11059200 | bytes 12165120 | tf_op jit(solution)/shard_map/concatenate | solution.py:70
  295.8 6.0 %fusion.14 = bf16[90,32,3,4,96]{4,1,3,2,0:T(8,128)(2,1)} fusion(bf16[90,16,3,4,96]{4,1,3,2,0:T(8,128)(2,1)} %collective-permute-done, bf16[90,16,3,4,96]{4,1,3,2,0:T(8,128)(2,1)S(1)} %copy-done, bf16[75,32,3,4,96]{4,1,3,2,0:T(8,128)(2,1)S(1)} %fusion.15), kind=kLoop, calls=%fused_computation.23 | loop fusion | flops 19906560 | bytes 18800640 | tf_op jit(solution)/shard_map/jit(_roll_static)/concatenate | solution.py:71
  301.8 9.0 %copy.36 = bf16[90,32,3,4,96]{4,1,0,3,2:T(8,128)(2,1)} copy(bf16[90,32,3,4,96]{4,1,3,2,0:T(8,128)(2,1)} %fusion.14) | data formatting | bytes 13271040 | tf_op jit(solution)/shard_map/jit(_roll_static)/concatenate | solution.py:71
  310.7 11.3 %copy.38 = bf16[3,960,3,4,96]{1,4,3,2,0:T(8,128)(2,1)} copy(bf16[3,960,3,4,96]{4,1,0,3,2:T(8,128)(2,1)} %bitcast.77) | data formatting | bytes 13271040 | tf_op jit(solution)/shard_map/while | solution.py:52
  322.0 59.7 %while.10 = (s32[]{:T(128)}, bf16[3,960,4,96]{1,3,2,0:T(8,128)(2,1)}, bf16[3,960,3,4,96]{1,4,3,2,0:T(8,128)(2,1)}, s32[3,960]{1,0:T(4,128)S(1)}, s32[]{:T(128)}) while((s32[]{:T(128)}, bf16[3,960,4,96]{1,3,2,0:T(8,128)(2,1)}, bf16[3,960,3,4,96]{1,4,3,2,0:T(8,128)(2,1)}, s32[3,960]{1,0:T(4,128)S(1)}, s32[]{:T(128)}) %tuple.26), condition=%wide.region_3.4_spmd, body=%wide.region_0.3_spmd.sunk | while | flops 1438987264 | bytes 39992132 | solution.py:52
  322.0 2.0 dynamic-slice_bitcast_fusion.2
  324.6 9.5 %fusion.27 = (f32[4,960]{1,0:T(4,128)S(1)}, f32[4,960,960]{1,2,0:T(8,128)}) fusion(pred[960,960]{0,1:T(8,128)(4,1)S(1)} %broadcast_compare_fusion.2, bf16[960,3,4,96]{0,3,2,1:T(8,128)(2,1)S(1)} %dynamic-slice_bitcast_fusion.2), kind=kOutput, calls=%fused_computation.38.clone.1 | convolution fusion | flops 722535360 | bytes 17316864 | tf_op jit(solution)/shard_map/while/body/eval_jaxpr/sub | solution.py:29
  334.1 7.7 %fusion.28 = bf16[3,960,4,96]{1,3,2,0:T(8,128)(2,1)} fusion(bf16[3,960,4,96]{1,3,2,0:T(8,128)(2,1)} %get-tuple-element.91, s32[]{:T(128)} %get-tuple-element.90, f32[4,960,960]{1,2,0:T(8,128)} %get-tuple-element.83, f32[4,960]{1,0:T(4,128)S(1)} %get-tuple-element.84, bf16[960,3,4,96]{0,3,2,1:T(8,128)(2,1)S(1)} %dynamic-slice_bitcast_fusion.2), kind=kOutput, calls=%fused_computation.14.clone.1 | convolution fusion | flops 715530240 | bytes 17318400 | tf_op jit(solution)/shard_map/while/body/eval_jaxpr/hqk,khd->qhd/dot_general | solution.py:31
  344.5 9.5 %fusion.27 = (f32[4,960]{1,0:T(4,128)S(1)}, f32[4,960,960]{1,2,0:T(8,128)}) fusion(pred[960,960]{0,1:T(8,128)(4,1)S(1)} %broadcast_compare_fusion.2, bf16[960,3,4,96]{0,3,2,1:T(8,128)(2,1)S(1)} %dynamic-slice_bitcast_fusion.2), kind=kOutput, calls=%fused_computation.38.clone.1 | convolution fusion | flops 722535360 | bytes 17316864 | tf_op jit(solution)/shard_map/while/body/eval_jaxpr/sub | solution.py:29
  354.0 7.8 %fusion.28 = bf16[3,960,4,96]{1,3,2,0:T(8,128)(2,1)} fusion(bf16[3,960,4,96]{1,3,2,0:T(8,128)(2,1)} %get-tuple-element.91, s32[]{:T(128)} %get-tuple-element.90, f32[4,960,960]{1,2,0:T(8,128)} %get-tuple-element.83, f32[4,960]{1,0:T(4,128)S(1)} %get-tuple-element.84, bf16[960,3,4,96]{0,3,2,1:T(8,128)(2,1)S(1)} %dynamic-slice_bitcast_fusion.2), kind=kOutput, calls=%fused_computation.14.clone.1 | convolution fusion | flops 715530240 | bytes 17318400 | tf_op jit(solution)/shard_map/while/body/eval_jaxpr/hqk,khd->qhd/dot_general | solution.py:31
  364.4 9.5 %fusion.27 = (f32[4,960]{1,0:T(4,128)S(1)}, f32[4,960,960]{1,2,0:T(8,128)}) fusion(pred[960,960]{0,1:T(8,128)(4,1)S(1)} %broadcast_compare_fusion.2, bf16[960,3,4,96]{0,3,2,1:T(8,128)(2,1)S(1)} %dynamic-slice_bitcast_fusion.2), kind=kOutput, calls=%fused_computation.38.clone.1 | convolution fusion | flops 722535360 | bytes 17316864 | tf_op jit(solution)/shard_map/while/body/eval_jaxpr/sub | solution.py:29
  373.9 7.8 %fusion.28 = bf16[3,960,4,96]{1,3,2,0:T(8,128)(2,1)} fusion(bf16[3,960,4,96]{1,3,2,0:T(8,128)(2,1)} %get-tuple-element.91, s32[]{:T(128)} %get-tuple-element.90, f32[4,960,960]{1,2,0:T(8,128)} %get-tuple-element.83, f32[4,960]{1,0:T(4,128)S(1)} %get-tuple-element.84, bf16[960,3,4,96]{0,3,2,1:T(8,128)(2,1)S(1)} %dynamic-slice_bitcast_fusion.2), kind=kOutput, calls=%fused_computation.14.clone.1 | convolution fusion | flops 715530240 | bytes 17318400 | tf_op jit(solution)/shard_map/while/body/eval_jaxpr/hqk,khd->qhd/dot_general | solution.py:31
  381.7 3.3 copy.39
  386.7 19.2 %collective-permute-done.1 = bf16[90,16,4,96]{3,1,0,2:T(8,128)(2,1)S(1)} collective-permute-done((bf16[90,16,4,96]{3,1,0,2:T(8,128)(2,1)S(1)}, bf16[90,16,4,96]{3,1,0,2:T(8,128)(2,1)S(1)}, u32[]{:S(2)}, u32[]{:S(2)}) %collective-permute-start.1) | collective-permute-done | bytes 1105952 | tf_op jit(solution)/shard_map/ppermute | solution.py:16
  406.5 2.3 copy.40
  408.7 66.9 %all_to_all.31 = bf16[90,1,32,1,4,96]{5,4,3,1,0,2:T(4,128)(2,1)S(1)} all-to-all(bf16[90,1,32,1,4,96]{5,4,3,1,0,2:T(4,128)(2,1)S(1)} %copy.40), channel_id=1, replica_groups=mesh['win'=8,'seq'=4] {'seq'}, dimensions={2} | all-to-all | bytes 4423680 | tf_op jit(solution)/shard_map/all_to_all | solution.py:77
  477.2 4.3 reshape_reshape.3
  481.6 8.6 %fusion.19 = bf16[90,1,8,1536]{3,2,1,0:T(8,128)(2,1)} fusion(bf16[720,1536]{1,0:T(8,128)(2,1)} %reshape_reshape.3, bf16[1536,1536]{1,0:T(8,128)(2,1)} %param.8, bf16[90,1,8,1536]{3,2,1,0:T(8,128)(2,1)} %param.7), kind=kOutput, calls=%fused_computation.36 | convolution fusion | flops 3400704000 | bytes 11354112 | tf_op jit(solution)/shard_map/dot_general | solution.py:79
  (22 shorter events, 11.1 us)
Async XLA Ops:
  231.4 10.4 %copy-start.1 = (s32[90,1,32]{0,2,1:T(8,128)S(1)}, s32[90,1,32]{0,2,1:T(8,128)}, u32[]{:S(2)}) copy-start(s32[90,1,32]{0,2,1:T(8,128)} %param.9) | copy-start | bytes 34564
  240.7 49.9 %collective-permute-start = (bf16[90,16,3,4,96]{4,1,3,2,0:T(8,128)(2,1)}, bf16[90,16,3,4,96]{4,1,3,2,0:T(8,128)(2,1)}, u32[]{:S(2)}, u32[]{:S(2)}) collective-permute-start(bf16[90,16,3,4,96]{4,1,3,2,0:T(8,128)(2,1)} %get-tuple-element.55), channel_id=1, source_target_pairs={{4,0},{8,4},{12,8},{16,12},{20,16},{24,20},{28,24},{0,28},{5,1},{9... | collective-permute-start | bytes 9953288 | tf_op jit(solution)/shard_map/ppermute | solution.py:16
  290.6 5.2 %copy-start = (bf16[90,16,3,4,96]{4,1,3,2,0:T(8,128)(2,1)S(1)}, bf16[90,16,3,4,96]{4,1,3,2,0:T(8,128)(2,1)}, u32[]{:S(2)}) copy-start(bf16[90,16,3,4,96]{4,1,3,2,0:T(8,128)(2,1)} %get-tuple-element.54) | copy-start | bytes 9953284
  385.8 20.1 %collective-permute-start.1 = (bf16[90,16,4,96]{3,1,0,2:T(8,128)(2,1)S(1)}, bf16[90,16,4,96]{3,1,0,2:T(8,128)(2,1)S(1)}, u32[]{:S(2)}, u32[]{:S(2)}) collective-permute-start(bf16[90,16,4,96]{3,1,0,2:T(8,128)(2,1)S(1)} %fusion.20), channel_id=1, source_target_pairs={{28,0},{0,4},{4,8},{8,12},{12,16},{16,20},{20,24},{24,28},{29,1},{... | collective-permute-start | bytes 3317768 | tf_op jit(solution)/shard_map/ppermute | solution.py:16
where the time goes:
time: 491 us; the launch traced here: 490 us
  blocking collectives  266 us (54%)
  local copies, waits for them, and re-layouts  80.1 us (16%)
  waiting for transfers between devices  67.8 us (14%)
  matrix products  60.3 us (12%)
  other arithmetic  13.8 us (3%)
    all_to_all x1, blocking collectives, per_device(): lax.all_to_all(split_heads, 'seq', split_axis=4, concat_axis=2, tiled=True)  199 us
    ppermute x2, waiting for transfers between devices, from_behind(): return lax.ppermute(block, axis, route)  67.8 us
    all_to_all x1, blocking collectives, per_device(): lax.all_to_all(attended, 'seq', split_axis=2, concat_axis=3, tiled=True)  66.9 us
    sub x3, matrix products, attend(): weights = jnp.exp(scores - largest)  28.4 us
    dot_general x3, matrix products, attend(): jnp.einsum('hqk,khd->qhd', soft_weights, values, preferred_element_type=j...  23.3 us
    reshape x2, local copies, waits for them, and re-layouts, per_device(): qkv_grid.reshape(lat_rows, win_count, col_count, 3, seq_count, group_head...  22.6 us
    while x2, local copies, waits for them, and re-layouts, window_attention(): attended = lax.map(one_window, (blocks, labels))  14.6 us
  transfers between devices with their start and end apart: 2, of which 2 were waited for; matrix products, arithmetic and copies ran while one was open for 0% of the time, Pallas kernels for 0%

commit v1 on v0

--- a/solution.py
+++ b/solution.py
@@ -64,7 +64,12 @@
     half_rows = WH // 2
     group_heads = HEADS // seq_count
     split_heads = qkv_grid.reshape(lat_rows, win_count, col_count, 3, seq_count, group_heads, HD)
-    gathered = lax.all_to_all(split_heads, "seq", split_axis=4, concat_axis=2, tiled=True)
+    gathered = jnp.concatenate(
+        lax.all_to_all(
+            jnp.stack(jnp.split(split_heads, lax.axis_size("seq"), axis=4)), "seq", 0, 0
+        ),
+        axis=2,
+    )
     flat_grid = gathered.reshape(lat_rows, win_count * WW, 3, group_heads, HD)
     arriving = from_behind(flat_grid[:, :half_cols], "win", -1)
     shifted = jnp.concatenate([flat_grid[:, half_cols:], arriving], axis=1)

time: 491 us -> 501 us (1.020)
  other arithmetic: 13.8 us -> 23.1 us
    all_to_all x1 -> x0, local copies, waits for them, and re-layouts: 9.7 us -> none  [per_device(): lax.all_to_all(split_heads, 'seq', split_axis=4, concat_axis=2, tiled=True)]
    reshape x0 -> x1, local copies, waits for them, and re-layouts: none -> 9.7 us  [per_device(): jnp.concatenate(lax.all_to_all(jnp.stack(jnp.split(split_heads, lax.axis_...]
    another operation x0 -> x1, other arithmetic: none -> 9.27 us  [per_device(): jnp.stack(jnp.split(split_heads, lax.axis_size('seq'), axis=4))]
    reshape x2 -> x1, local copies, waits for them, and re-layouts: 22.6 us -> 17 us  [per_device(): qkv_grid.reshape(lat_rows, win_count, col_count, 3, seq_count, group_head...]
    another operation x0 -> x1, local copies, waits for them, and re-layouts: none -> 5.51 us  [per_device(): jnp.stack(jnp.split(split_heads, lax.axis_size('seq'), axis=4))]
where the time goes in v1:
time: 501 us; the launch traced here: 500 us
  blocking collectives  266 us (53%)
  local copies, waits for them, and re-layouts  80.1 us (16%)
  waiting for transfers between devices  67.8 us (14%)
  matrix products  60.4 us (12%)
  other arithmetic  23.1 us (5%)
    all_to_all x1, blocking collectives, per_device(): lax.all_to_all(jnp.stack(jnp.split(split_heads, lax.axis_size('seq'), axi...  199 us
    ppermute x2, waiting for transfers between devices, from_behind(): return lax.ppermute(block, axis, route)  67.8 us
    all_to_all x1, blocking collectives, per_device(): lax.all_to_all(attended, 'seq', split_axis=2, concat_axis=3, tiled=True)  66.9 us
    sub x3, matrix products, attend(): weights = jnp.exp(scores - largest)  28.5 us
    dot_general x3, matrix products, attend(): jnp.einsum('hqk,khd->qhd', soft_weights, values, preferred_element_type=j...  23.3 us
    reshape x1, local copies, waits for them, and re-layouts, per_device(): qkv_grid.reshape(lat_rows, win_count, col_count, 3, seq_count, group_head...  17 us
    while x2, local copies, waits for them, and re-layouts, window_attention(): attended = lax.map(one_window, (blocks, labels))  14.6 us
  transfers between devices with their start and end apart: 2, of which 2 were waited for; matrix products, arithmetic and copies ran while one was open for 0% of the time, Pallas kernels for 0%

profile of v1, /device:TPU:0, one launch (start us, length us, event | category | flops | bytes accessed | tf_op | source)
XLA Modules:
  0.0 499.5 jit_solution(17035862254099834257)
XLA Ops:
  0.0 17.0 %reshape.49 = bf16[90,1,8,3,4,4,96]{6,5,4,3,2,0,1:T(4,128)(2,1)} reshape(bf16[90,1,8,4608]{3,2,1,0:T(8,128)(2,1)} %param.6) | data formatting | bytes 13271040 | tf_op jit(solution)/shard_map/reshape | solution.py:66
  17.0 5.5 %slice_bitcast_fusion.17 = (bf16[1,90,1,8,3,1,4,96]{7,6,4,3,1,5,2,0:T(4,128)(2,1)S(1)}, bf16[1,90,1,8,3,1,4,96]{7,6,4,3,1,5,2,0:T(4,128)(2,1)S(1)}, bf16[1,90,1,...) fusion(bf16[90,1,8,3,4,4,96]{6,5,4,3,2,0,1:T(4,128)(2,1)} %reshape.49), kind=kLoop, calls=%fused_computation.41 | loop fusion | bytes 13271040 | tf_op jit(solution)/shard_map/stack | solution.py:69
  22.6 9.3 %pad_maximum_fusion.1 = bf16[4,90,1,8,3,1,4,96]{7,6,4,3,1,5,2,0:T(4,128)(2,1)S(1)} fusion(bf16[1,90,1,8,3,1,4,96]{7,6,4,3,1,5,2,0:T(4,128)(2,1)S(1)} %get-tuple-element.58, bf16[1,90,1,8,3,1,4,96]{7,6,4,3,1,5,2,0:T(4,128)(2,1)S(1)} %get-tuple-element.59, bf16[1,90,1,8,3,1,4,96]{7,6,4,3,1,5,2,0:T(4,128)(2,1)S(1)} %get-tuple-element.57, ...), kind=kLoop, calls=%fused_computation.24 | loop fusion | flops 9953280 | bytes 13271040 | tf_op jit(solution)/shard_map/stack | solution.py:69
  31.8 199.1 %all_to_all.20 = bf16[4,90,1,8,3,1,4,96]{7,6,4,3,1,5,2,0:T(4,128)(2,1)} all-to-all(bf16[4,90,1,8,3,1,4,96]{7,6,4,3,1,5,2,0:T(4,128)(2,1)S(1)} %pad_maximum_fusion.1), channel_id=1, replica_groups=mesh['win'=8,'seq'=4] {'seq'}, dimensions={0} | all-to-all | bytes 13271040 | tf_op jit(solution)/shard_map/all_to_all | solution.py:68
  230.9 9.7 %copy.62 = bf16[90,1,4,8,3,1,4,96]{7,3,2,6,4,0,5,1:T(8,128)(2,1)} copy(bf16[90,1,4,8,3,1,4,96]{7,6,4,3,0,5,1,2:T(4,128)(2,1)} %bitcast.88) | data formatting | bytes 13271040 | tf_op jit(solution)/shard_map/reshape | solution.py:67
  240.6 9.3 %fusion.22 = (bf16[90,16,3,4,96]{4,1,3,2,0:T(8,128)(2,1)}, bf16[90,16,3,4,96]{4,1,3,2,0:T(8,128)(2,1)}) fusion(bf16[90,32,3,4,96]{4,1,3,2,0:T(8,128)(2,1)} %bitcast.87), kind=kLoop, calls=%fused_computation.44 | loop fusion | bytes 13271040 | tf_op jit(solution)/shard_map/slice | solution.py:75
  251.3 48.6 %collective-permute-done = bf16[90,16,3,4,96]{4,1,3,2,0:T(8,128)(2,1)} collective-permute-done((bf16[90,16,3,4,96]{4,1,3,2,0:T(8,128)(2,1)}, bf16[90,16,3,4,96]{4,1,3,2,0:T(8,128)(2,1)}, u32[]{:S(2)}, u32[]{:S(2)}) %collective-permute-start) | collective-permute-done | bytes 3317792 | tf_op jit(solution)/shard_map/ppermute | solution.py:16
  299.9 5.2 %fusion.15 = bf16[75,32,3,4,96]{4,1,3,2,0:T(8,128)(2,1)S(1)} fusion(bf16[90,16,3,4,96]{4,1,3,2,0:T(8,128)(2,1)} %get-tuple-element.54, bf16[90,16,3,4,96]{4,1,3,2,0:T(8,128)(2,1)} %collective-permute-done), kind=kLoop, calls=%fused_computation.28 | loop fusion | flops 11059200 | bytes 12165120 | tf_op jit(solution)/shard_map/concatenate | solution.py:75
  305.1 6.0 %fusion.14 = bf16[90,32,3,4,96]{4,1,3,2,0:T(8,128)(2,1)} fusion(bf16[90,16,3,4,96]{4,1,3,2,0:T(8,128)(2,1)} %collective-permute-done, bf16[90,16,3,4,96]{4,1,3,2,0:T(8,128)(2,1)S(1)} %copy-done, bf16[75,32,3,4,96]{4,1,3,2,0:T(8,128)(2,1)S(1)} %fusion.15), kind=kLoop, calls=%fused_computation.23 | loop fusion | flops 19906560 | bytes 18800640 | tf_op jit(solution)/shard_map/jit(_roll_static)/concatenate | solution.py:76
  311.0 9.0 %copy.49 = bf16[90,32,3,4,96]{4,1,0,3,2:T(8,128)(2,1)} copy(bf16[90,32,3,4,96]{4,1,3,2,0:T(8,128)(2,1)} %fusion.14) | data formatting | bytes 13271040 | tf_op jit(solution)/shard_map/jit(_roll_static)/concatenate | solution.py:76
  320.0 11.3 %copy.51 = bf16[3,960,3,4,96]{1,4,3,2,0:T(8,128)(2,1)} copy(bf16[3,960,3,4,96]{4,1,0,3,2:T(8,128)(2,1)} %bitcast.89) | data formatting | bytes 13271040 | tf_op jit(solution)/shard_map/while | solution.py:52
  331.3 59.8 %while.10 = (s32[]{:T(128)}, bf16[3,960,4,96]{1,3,2,0:T(8,128)(2,1)}, bf16[3,960,3,4,96]{1,4,3,2,0:T(8,128)(2,1)}, s32[3,960]{1,0:T(4,128)S(1)}, s32[]{:T(128)}) while((s32[]{:T(128)}, bf16[3,960,4,96]{1,3,2,0:T(8,128)(2,1)}, bf16[3,960,3,4,96]{1,4,3,2,0:T(8,128)(2,1)}, s32[3,960]{1,0:T(4,128)S(1)}, s32[]{:T(128)}) %tuple.29), condition=%wide.region_3.4_spmd, body=%wide.region_0.3_spmd.sunk | while | flops 1438987264 | bytes 39992132 | solution.py:52
  333.9 9.5 %fusion.27 = (f32[4,960]{1,0:T(4,128)S(1)}, f32[4,960,960]{1,2,0:T(8,128)}) fusion(pred[960,960]{0,1:T(8,128)(4,1)S(1)} %broadcast_compare_fusion.2, bf16[960,3,4,96]{0,3,2,1:T(8,128)(2,1)S(1)} %dynamic-slice_bitcast_fusion.2), kind=kOutput, calls=%fused_computation.43.clone.1 | convolution fusion | flops 722535360 | bytes 17316864 | tf_op jit(solution)/shard_map/while/body/eval_jaxpr/sub | solution.py:29
  343.4 7.8 %fusion.28 = bf16[3,960,4,96]{1,3,2,0:T(8,128)(2,1)} fusion(bf16[3,960,4,96]{1,3,2,0:T(8,128)(2,1)} %get-tuple-element.95, s32[]{:T(128)} %get-tuple-element.94, f32[4,960,960]{1,2,0:T(8,128)} %get-tuple-element.87, f32[4,960]{1,0:T(4,128)S(1)} %get-tuple-element.88, bf16[960,3,4,96]{0,3,2,1:T(8,128)(2,1)S(1)} %dynamic-slice_bitcast_fusion.2), kind=kOutput, calls=%fused_computation.14.clone.1 | convolution fusion | flops 715530240 | bytes 17318400 | tf_op jit(solution)/shard_map/while/body/eval_jaxpr/hqk,khd->qhd/dot_general | solution.py:31
  353.9 9.5 %fusion.27 = (f32[4,960]{1,0:T(4,128)S(1)}, f32[4,960,960]{1,2,0:T(8,128)}) fusion(pred[960,960]{0,1:T(8,128)(4,1)S(1)} %broadcast_compare_fusion.2, bf16[960,3,4,96]{0,3,2,1:T(8,128)(2,1)S(1)} %dynamic-slice_bitcast_fusion.2), kind=kOutput, calls=%fused_computation.43.clone.1 | convolution fusion | flops 722535360 | bytes 17316864 | tf_op jit(solution)/shard_map/while/body/eval_jaxpr/sub | solution.py:29
  363.3 7.8 %fusion.28 = bf16[3,960,4,96]{1,3,2,0:T(8,128)(2,1)} fusion(bf16[3,960,4,96]{1,3,2,0:T(8,128)(2,1)} %get-tuple-element.95, s32[]{:T(128)} %get-tuple-element.94, f32[4,960,960]{1,2,0:T(8,128)} %get-tuple-element.87, f32[4,960]{1,0:T(4,128)S(1)} %get-tuple-element.88, bf16[960,3,4,96]{0,3,2,1:T(8,128)(2,1)S(1)} %dynamic-slice_bitcast_fusion.2), kind=kOutput, calls=%fused_computation.14.clone.1 | convolution fusion | flops 715530240 | bytes 17318400 | tf_op jit(solution)/shard_map/while/body/eval_jaxpr/hqk,khd->qhd/dot_general | solution.py:31
  373.8 9.5 %fusion.27 = (f32[4,960]{1,0:T(4,128)S(1)}, f32[4,960,960]{1,2,0:T(8,128)}) fusion(pred[960,960]{0,1:T(8,128)(4,1)S(1)} %broadcast_compare_fusion.2, bf16[960,3,4,96]{0,3,2,1:T(8,128)(2,1)S(1)} %dynamic-slice_bitcast_fusion.2), kind=kOutput, calls=%fused_computation.43.clone.1 | convolution fusion | flops 722535360 | bytes 17316864 | tf_op jit(solution)/shard_map/while/body/eval_jaxpr/sub | solution.py:29
  383.3 7.8 %fusion.28 = bf16[3,960,4,96]{1,3,2,0:T(8,128)(2,1)} fusion(bf16[3,960,4,96]{1,3,2,0:T(8,128)(2,1)} %get-tuple-element.95, s32[]{:T(128)} %get-tuple-element.94, f32[4,960,960]{1,2,0:T(8,128)} %get-tuple-element.87, f32[4,960]{1,0:T(4,128)S(1)} %get-tuple-element.88, bf16[960,3,4,96]{0,3,2,1:T(8,128)(2,1)S(1)} %dynamic-slice_bitcast_fusion.2), kind=kOutput, calls=%fused_computation.14.clone.1 | convolution fusion | flops 715530240 | bytes 17318400 | tf_op jit(solution)/shard_map/while/body/eval_jaxpr/hqk,khd->qhd/dot_general | solution.py:31
  391.0 3.3 copy.52
  396.0 19.2 %collective-permute-done.1 = bf16[90,16,4,96]{3,1,0,2:T(8,128)(2,1)S(1)} collective-permute-done((bf16[90,16,4,96]{3,1,0,2:T(8,128)(2,1)S(1)}, bf16[90,16,4,96]{3,1,0,2:T(8,128)(2,1)S(1)}, u32[]{:S(2)}, u32[]{:S(2)}) %collective-permute-start.1) | collective-permute-done | bytes 1105952 | tf_op jit(solution)/shard_map/ppermute | solution.py:16
  415.8 2.3 copy.53
  418.1 66.9 %all_to_all.21 = bf16[90,1,32,1,4,96]{5,4,3,1,0,2:T(4,128)(2,1)S(1)} all-to-all(bf16[90,1,32,1,4,96]{5,4,3,1,0,2:T(4,128)(2,1)S(1)} %copy.53), channel_id=1, replica_groups=mesh['win'=8,'seq'=4] {'seq'}, dimensions={2} | all-to-all | bytes 4423680 | tf_op jit(solution)/shard_map/all_to_all | solution.py:82
  486.6 4.3 reshape_reshape.7
  490.9 8.6 %fusion.19 = bf16[90,1,8,1536]{3,2,1,0:T(8,128)(2,1)} fusion(bf16[720,1536]{1,0:T(8,128)(2,1)} %reshape_reshape.7, bf16[1536,1536]{1,0:T(8,128)(2,1)} %param.8, bf16[90,1,8,1536]{3,2,1,0:T(8,128)(2,1)} %param.7), kind=kOutput, calls=%fused_computation.37 | convolution fusion | flops 3400704000 | bytes 11354112 | tf_op jit(solution)/shard_map/dot_general | solution.py:84
  (23 shorter events, 13.2 us)
Async XLA Ops:
  240.6 10.4 %copy-start.1 = (s32[90,1,32]{0,2,1:T(8,128)S(1)}, s32[90,1,32]{0,2,1:T(8,128)}, u32[]{:S(2)}) copy-start(s32[90,1,32]{0,2,1:T(8,128)} %param.9) | copy-start | bytes 34564
  250.0 49.9 %collective-permute-start = (bf16[90,16,3,4,96]{4,1,3,2,0:T(8,128)(2,1)}, bf16[90,16,3,4,96]{4,1,3,2,0:T(8,128)(2,1)}, u32[]{:S(2)}, u32[]{:S(2)}) collective-permute-start(bf16[90,16,3,4,96]{4,1,3,2,0:T(8,128)(2,1)} %get-tuple-element.55), channel_id=1, source_target_pairs={{4,0},{8,4},{12,8},{16,12},{20,16},{24,20},{28,24},{0,28},{5,1},{9... | collective-permute-start | bytes 9953288 | tf_op jit(solution)/shard_map/ppermute | solution.py:16
  299.9 5.2 %copy-start = (bf16[90,16,3,4,96]{4,1,3,2,0:T(8,128)(2,1)S(1)}, bf16[90,16,3,4,96]{4,1,3,2,0:T(8,128)(2,1)}, u32[]{:S(2)}) copy-start(bf16[90,16,3,4,96]{4,1,3,2,0:T(8,128)(2,1)} %get-tuple-element.54) | copy-start | bytes 9953284
  395.1 20.1 %collective-permute-start.1 = (bf16[90,16,4,96]{3,1,0,2:T(8,128)(2,1)S(1)}, bf16[90,16,4,96]{3,1,0,2:T(8,128)(2,1)S(1)}, u32[]{:S(2)}, u32[]{:S(2)}) collective-permute-start(bf16[90,16,4,96]{3,1,0,2:T(8,128)(2,1)S(1)} %fusion.20), channel_id=1, source_target_pairs={{28,0},{0,4},{4,8},{8,12},{12,16},{16,20},{20,24},{24,28},{29,1},{... | collective-permute-start | bytes 3317768 | tf_op jit(solution)/shard_map/ppermute | solution.py:16
